TPU v7x, 32 devices: a whole 2x2x4 slice. The times are simulated.
32 devices in a mesh: dp: 8 (over z, x), tp: 4 (over y, core).
Axes of the slice: x: 2, y: 2, z: 4, core: 2. Of those that a mesh axis runs over, the one named last changes fastest.
Arguments:
- layer_input: bfloat16 [8, 1024, 768], P('dp', 'tp'), may hold values from -6 to 6
- lengths: int32 [8], P('dp'), may hold values from 8 to 1024, as said below
- w_qkv: bfloat16 [768, 3, 768], P(None, None, 'tp'), may hold values from -0.21875 to 0.21875
- w_out: bfloat16 [768, 768], P('tp'), may hold values from -1.75 to 1.75
- w_gate: bfloat16 [768, 3072], P(None, 'tp'), may hold values from -0.21875 to 0.21875
- w_up: bfloat16 [768, 3072], P(None, 'tp'), may hold values from -0.21875 to 0.21875
- w_down: bfloat16 [3072, 768], P('tp'), may hold values from -0.109375 to 0.109375
- gain_one: float32 [768], replicated, may hold values from 0.5 to 1.5
- bias_one: float32 [768], replicated, may hold values from -1.8 to 1.8
- gain_two: float32 [768], replicated, may hold values from 0.5 to 1.5
- bias_two: float32 [768], replicated, may hold values from -1.8 to 1.8
- cotangent: bfloat16 [8, 1024, 768], P('dp', 'tp'), may hold values from -6 to 6
Outputs:
- output: bfloat16 [8, 1024, 768], P('dp', 'tp')
- input_grad: float32 [8, 1024, 768], P('dp', 'tp')
- qkv_grad: float32 [768, 3, 768], P('dp', None, 'tp')
- out_grad: float32 [768, 768], P('tp', 'dp')
- gate_grad: float32 [768, 3072], P('dp', 'tp')
- up_grad: float32 [768, 3072], P('dp', 'tp')
- down_grad: float32 [3072, 768], P('tp', 'dp')
- gain_one_grad: float32 [768], replicated
- bias_one_grad: float32 [768], replicated
- gain_two_grad: float32 [768], replicated
- bias_two_grad: float32 [768], replicated
Inputs may be any that keep to these rules, and one draw needn't show every extreme that they name: `lengths`: each row's count of real tokens; later positions of the row are padding. Some row has exactly 1024 and some row exactly 8.
All inputs are finite; a program needn't handle non-finite values.
Results may differ from a plain program's by a relative error of at most 0.017.
Values may be sent and summed in bfloat16 or wider, within the bound.
No kernel may reach another device: no remote copies, remote signals or barrier semaphores. Data moves between devices by JAX's collectives and lax.ppermute only.
A program may use at most 128 MiB of HBM per device.

v0:
```python
import jax
import jax.numpy as jnp
from jax import lax
from jax.sharding import PartitionSpec as P

HD = 64
masked_score = -1e30
epsilon = 1e-05


def angle_tables(positions_count, head_width):
    position = jnp.arange(positions_count, dtype=jnp.float32)
    frequency = 1000.0 ** (-jnp.arange(head_width // 2, dtype=jnp.float32) * 2.0 / head_width)
    angles = position[:, None] * frequency[None, :]
    return (jnp.cos(angles)[:, None, :], jnp.sin(angles)[:, None, :])


def rotate(values, cosine, sine_table, direction):
    half_width = values.shape[-1] // 2
    lower = values[..., :half_width]
    upper = values[..., half_width:]
    return jnp.concatenate(
        [
            lower * cosine - direction * upper * sine_table,
            upper * cosine + direction * lower * sine_table,
        ],
        axis=-1,
    )


def norm_forward(values, gain_vec, bias_vec):
    center = values - jnp.mean(values, axis=-1, keepdims=True)
    inverse = lax.rsqrt(jnp.mean(center * center, axis=-1, keepdims=True) + epsilon)
    normed = center * inverse
    return (normed * gain_vec + bias_vec, normed, inverse)


def norm_backward(upstream, normed, inverse, gain_vec):
    scaled = upstream * gain_vec
    grad_values = inverse * (
        scaled
        - jnp.mean(scaled, axis=-1, keepdims=True)
        - normed * jnp.mean(scaled * normed, axis=-1, keepdims=True)
    )
    gain_part = jnp.sum(upstream * normed, axis=(0, 1))
    bias_part = jnp.sum(upstream, axis=(0, 1))
    return (grad_values, gain_part, bias_part)


def body(
    layer_input,
    lengths,
    w_qkv,
    w_out,
    w_gate,
    w_up,
    w_down,
    gain_one,
    bias_one,
    gain_two,
    bias_two,
    cotangent,
):
    row_count, piece_len, model_width = layer_input.shape
    local_width = w_qkv.shape[2]
    heads_local = local_width // HD
    seq_len = piece_len * lax.axis_size("tp")
    offset = lax.axis_index("tp") * piece_len
    scale = HD ** (-0.5)
    key_valid = jnp.arange(seq_len, dtype=jnp.int32)[None, :] < lengths[:, None]
    own_positions = offset + jnp.arange(piece_len, dtype=jnp.int32)
    row_valid = (own_positions[None, :] < lengths[:, None]).astype(jnp.float32)
    cosine, sine_table = angle_tables(seq_len, HD)
    gathered = lax.all_gather(layer_input, "tp", axis=1, tiled=True)
    projected = jnp.einsum("rsd,dce->rsce", gathered, w_qkv, preferred_element_type=jnp.float32)
    shaped = projected.reshape(row_count, seq_len, 3, heads_local, HD)
    queries = rotate(shaped[:, :, 0], cosine, sine_table, 1.0).astype(jnp.bfloat16)
    keys_rot = rotate(shaped[:, :, 1], cosine, sine_table, 1.0).astype(jnp.bfloat16)
    values_low = shaped[:, :, 2].astype(jnp.bfloat16)

    def attend(operands):
        query_row, keys_row, values_row, valid_row = operands
        scores = (
            jnp.einsum("she,the->hst", query_row, keys_row, preferred_element_type=jnp.float32)
            * scale
        )
        scores = jnp.where(valid_row[None, None, :], scores, masked_score)
        row_max = jnp.max(scores, axis=-1, keepdims=True)
        exps_raw = jnp.exp(scores - row_max)
        row_total = jnp.sum(exps_raw, axis=-1, keepdims=True)
        attn_probs = (exps_raw / row_total).astype(jnp.bfloat16)
        mixed = jnp.einsum(
            "hst,the->she", attn_probs, values_row, preferred_element_type=jnp.float32
        )
        return (mixed.astype(jnp.bfloat16), (row_max + jnp.log(row_total))[..., 0])

    heads_out, log_total = lax.map(attend, (queries, keys_rot, values_low, key_valid))
    heads_flat = heads_out.reshape(row_count, seq_len, local_width)
    attn_partial = jnp.einsum("rsk,kd->rsd", heads_flat, w_out, preferred_element_type=jnp.float32)
    attn_out = lax.psum_scatter(attn_partial, "tp", scatter_dimension=1, tiled=True)
    first_norm, normed_one, inverse_one = norm_forward(
        layer_input.astype(jnp.float32) + attn_out, gain_one, bias_one
    )
    first_low = first_norm.astype(jnp.bfloat16)
    gate_full, up_full, down_full = (w_gate, w_up, w_down)
    ffn_input = lax.all_gather(first_low, "tp", axis=1, tiled=True)
    gate_act = jnp.einsum("rsd,df->rsf", ffn_input, gate_full, preferred_element_type=jnp.float32)
    up_act = jnp.einsum("rsd,df->rsf", ffn_input, up_full, preferred_element_type=jnp.float32)
    sigmoid_gate = jax.nn.sigmoid(gate_act)
    hidden = (gate_act * sigmoid_gate * up_act).astype(jnp.bfloat16)
    ffn_partial = jnp.einsum("rsf,fd->rsd", hidden, down_full, preferred_element_type=jnp.float32)
    ffn_out = lax.psum_scatter(
        ffn_partial.astype(jnp.bfloat16), "tp", scatter_dimension=1, tiled=True
    ).astype(jnp.float32)
    second_out, normed_two, inverse_two = norm_forward(first_norm + ffn_out, gain_two, bias_two)
    output = (second_out * row_valid[:, :, None]).astype(jnp.bfloat16)
    grad_output = cotangent.astype(jnp.float32) * row_valid[:, :, None]
    grad_second, gain_two_part, bias_two_part = norm_backward(
        grad_output, normed_two, inverse_two, gain_two
    )
    grad_second_low = grad_second.astype(jnp.bfloat16)
    grad_ffn = lax.all_gather(grad_second_low, "tp", axis=1, tiled=True)
    down_grad = jnp.einsum("rsf,rsd->fd", hidden, grad_ffn, preferred_element_type=jnp.float32)
    grad_hidden = jnp.einsum("rsd,fd->rsf", grad_ffn, down_full, preferred_element_type=jnp.float32)
    grad_gate = (
        grad_hidden * up_act * sigmoid_gate * (1.0 + gate_act * (1.0 - sigmoid_gate))
    ).astype(jnp.bfloat16)
    grad_up = (grad_hidden * gate_act * sigmoid_gate).astype(jnp.bfloat16)
    gate_grad = jnp.einsum("rsd,rsf->df", ffn_input, grad_gate, preferred_element_type=jnp.float32)
    up_grad = jnp.einsum("rsd,rsf->df", ffn_input, grad_up, preferred_element_type=jnp.float32)
    grad_inner = jnp.einsum(
        "rsf,df->rsd", grad_gate, gate_full, preferred_element_type=jnp.float32
    ) + jnp.einsum("rsf,df->rsd", grad_up, up_full, preferred_element_type=jnp.float32)
    grad_first_part = lax.psum_scatter(grad_inner, "tp", scatter_dimension=1, tiled=True)
    grad_first = grad_second + grad_first_part
    grad_res, gain_one_part, bias_one_part = norm_backward(
        grad_first, normed_one, inverse_one, gain_one
    )
    grad_attn = lax.all_gather(grad_res.astype(jnp.bfloat16), "tp", axis=1, tiled=True)
    out_grad = jnp.einsum("rsk,rsd->kd", heads_flat, grad_attn, preferred_element_type=jnp.float32)
    grad_heads = jnp.einsum("rsd,kd->rsk", grad_attn, w_out, preferred_element_type=jnp.float32)
    grad_heads = grad_heads.astype(jnp.bfloat16).reshape(row_count, seq_len, heads_local, HD)

    def attend_back(operands):
        query_row, keys_row, values_row, valid_row, total_row, grad_row = operands
        scores = (
            jnp.einsum("she,the->hst", query_row, keys_row, preferred_element_type=jnp.float32)
            * scale
        )
        scores = jnp.where(valid_row[None, None, :], scores, masked_score)
        attn_probs = jnp.exp(scores - total_row[:, :, None])
        grad_probs = jnp.einsum(
            "she,the->hst", grad_row, values_row, preferred_element_type=jnp.float32
        )
        delta = jnp.sum(attn_probs * grad_probs, axis=-1, keepdims=True)
        grad_scores = (attn_probs * (grad_probs - delta)).astype(jnp.bfloat16)
        grad_query = (
            jnp.einsum("hst,the->she", grad_scores, keys_row, preferred_element_type=jnp.float32)
            * scale
        )
        grad_keys = (
            jnp.einsum("hst,she->the", grad_scores, query_row, preferred_element_type=jnp.float32)
            * scale
        )
        grad_values = jnp.einsum(
            "hst,she->the",
            attn_probs.astype(jnp.bfloat16),
            grad_row,
            preferred_element_type=jnp.float32,
        )
        return (grad_query, grad_keys, grad_values)

    grad_query, grad_keys, grad_values = lax.map(
        attend_back, (queries, keys_rot, values_low, key_valid, log_total, grad_heads)
    )
    grad_qkv = jnp.stack(
        [
            rotate(grad_query, cosine, sine_table, -1.0),
            rotate(grad_keys, cosine, sine_table, -1.0),
            grad_values,
        ],
        axis=2,
    )
    grad_qkv = grad_qkv.reshape(row_count, seq_len, 3, local_width).astype(jnp.bfloat16)
    qkv_grad = jnp.einsum("rsd,rsce->dce", gathered, grad_qkv, preferred_element_type=jnp.float32)
    grad_gathered = jnp.einsum("rsce,dce->rsd", grad_qkv, w_qkv, preferred_element_type=jnp.float32)
    input_grad = grad_res + lax.psum_scatter(
        grad_gathered.astype(jnp.bfloat16), "tp", scatter_dimension=1, tiled=True
    ).astype(jnp.float32)
    qkv_grad, out_grad, gate_grad, up_grad, down_grad = (
        lax.psum_scatter(qkv_grad, "dp", scatter_dimension=0, tiled=True),
        lax.psum_scatter(out_grad, "dp", scatter_dimension=1, tiled=True),
        lax.psum_scatter(gate_grad, "dp", scatter_dimension=0, tiled=True),
        lax.psum_scatter(up_grad, "dp", scatter_dimension=0, tiled=True),
        lax.psum_scatter(down_grad, "dp", scatter_dimension=1, tiled=True),
    )
    gain_one_grad, bias_one_grad, gain_two_grad, bias_two_grad = lax.psum(
        (gain_one_part, bias_one_part, gain_two_part, bias_two_part), ("dp", "tp")
    )
    return (
        output,
        input_grad,
        qkv_grad,
        out_grad,
        gate_grad,
        up_grad,
        down_grad,
        gain_one_grad,
        bias_one_grad,
        gain_two_grad,
        bias_two_grad,
    )


def solution(mesh):
    placed = (
        P("dp", "tp", None),
        P("dp"),
        P(None, None, "tp"),
        P("tp", None),
        P(None, "tp"),
        P(None, "tp"),
        P("tp", None),
        P(),
        P(),
        P(),
        P(),
        P("dp", "tp", None),
    )
    return jax.shard_map(
        body,
        mesh=mesh,
        in_specs=placed,
        out_specs=(
            P("dp", "tp", None),
            P("dp", "tp", None),
            P("dp", None, "tp"),
            P("tp", "dp"),
            P("dp", "tp"),
            P("dp", "tp"),
            P("tp", "dp"),
            P(),
            P(),
            P(),
            P(),
        ),
        check_vma=False,
    )
```

profile of v0, /device:TPU:0, one launch (start us, length us, event | category | flops | bytes accessed | tf_op | source)
XLA Modules:
  0.0 658.0 jit_solution(8090936462190204073)
XLA Ops:
  7.2 0.7 all-gather.5.cloned.1.call-update
  8.6 1.2 broadcast_multiply_fusion
  9.8 22.1 %all-gather.5.cloned.1.call-done = bf16[1,1024,768]{2,1,0:T(8,128)(2,1)} async-done(((bf16[1,256,768]{2,1,0:T(8,128)(2,1)}), bf16[1,1024,768]{2,1,0:T(8,128)(2,1)}) %all-gather.5.cloned.1.call-update) | async-done | bytes 1572880 | tf_op jit(solution)/shard_map/all_gather | solution.py:74
  32.0 2.7 convolution_bitcast_fusion.1
  34.8 0.2 fusion.44
  35.1 2.4 fusion.64
  37.5 1.7 fusion
  39.3 2.8 copy-done.2
  42.1 2.3 fusion.38
  44.5 0.7 copy-done.16
  45.2 2.3 convolution_bitcast_fusion
  47.5 38.0 %reduce-scatter.14.cloned.1.call-done = f32[1,256,768]{2,1,0:T(8,128)} async-done(((f32[1,1024,768]{2,1,0:T(8,128)}), f32[1,256,768]{2,1,0:T(8,128)}) %reduce-scatter.14.cloned.1.call-update) | async-done | bytes 786448 | tf_op jit(solution)/shard_map/reduce_scatter | solution.py:100
  85.5 1.3 fusion.63
  87.1 0.9 fusion.42
  88.1 19.7 %all-gather.7.cloned.1.call-done = bf16[1,1024,768]{2,1,0:T(8,128)(2,1)} async-done(((bf16[1,256,768]{2,1,0:T(8,128)(2,1)}), bf16[1,1024,768]{2,1,0:T(8,128)(2,1)}) %all-gather.7.cloned.1.call-update) | async-done | bytes 1572880 | tf_op jit(solution)/shard_map/all_gather | solution.py:106
  107.9 3.3 fusion.23
  111.2 5.4 multiply_convert_fusion.3
  116.6 1.2 copy-done.45
  117.8 2.5 fusion.25
  120.4 0.2 all-gather.9.cloned.1.call-start
  120.6 27.9 %reduce-scatter.16.cloned.1.call-done = bf16[1,256,768]{2,1,0:T(8,128)(2,1)} async-done(((bf16[1,1024,768]{2,1,0:T(8,128)(2,1)}), bf16[1,256,768]{2,1,0:T(8,128)(2,1)}) %reduce-scatter.16.cloned.1.call-update) | async-done | bytes 393232 | tf_op jit(solution)/shard_map/reduce_scatter | solution.py:112
  148.5 1.3 fusion.62
  149.9 0.2 multiply_reduce_fusion.5
  150.1 1.0 multiply_reduce_fusion.1
  151.1 1.1 fusion.59
  152.3 19.7 %all-gather.9.cloned.1.call-done = bf16[1,1024,768]{2,1,0:T(8,128)(2,1)} async-done(((bf16[1,256,768]{2,1,0:T(8,128)(2,1)}), bf16[1,1024,768]{2,1,0:T(8,128)(2,1)}) %all-gather.9.cloned.1.call-update) | async-done | bytes 1572880 | tf_op jit(solution)/shard_map/all_gather | solution.py:122
  172.0 5.4 multiply_convert_fusion.1
  177.5 1.4 fusion.65
  179.1 0.5 copy-done.20
  179.6 3.1 add_bitcast_fusion
  182.8 38.0 %reduce-scatter.18.cloned.1.call-done = f32[1,256,768]{2,1,0:T(8,128)} async-done(((f32[1,1024,768]{2,1,0:T(8,128)}), f32[1,256,768]{2,1,0:T(8,128)}) %reduce-scatter.18.cloned.1.call-update) | async-done | bytes 786448 | tf_op jit(solution)/shard_map/reduce_scatter | solution.py:134
  220.8 3.2 multiply_reduce_fusion.2
  224.0 1.7 fusion.60
  225.9 19.7 %all-gather.11.cloned.1.call-done = bf16[1,1024,768]{2,1,0:T(8,128)(2,1)} async-done(((bf16[1,256,768]{2,1,0:T(8,128)(2,1)}), bf16[1,1024,768]{2,1,0:T(8,128)(2,1)}) %all-gather.11.cloned.1.call-update) | async-done | bytes 1572880 | tf_op jit(solution)/shard_map/all_gather | solution.py:139
  245.6 2.1 fusion.32
  247.7 6.3 multiply_reduce_fusion
  254.0 1.0 slice-done.1
  255.0 1.2 slice-done.2
  256.2 5.3 multiply_convert_fusion
  261.5 5.0 fusion.27
  266.5 1.2 fusion.28
  267.9 1.6 fusion.29
  269.6 0.2 subtract_convert_fusion.1
  270.0 6.7 %fusion.35 = bf16[3,64,1024]{2,1,0:T(8,128)(2,1)S(1)} fusion(bf16[1024,3,64]{0,2,1:T(8,128)(2,1)S(1)} %bitcast.125, f32[3,1024,1024]{1,2,0:T(8,128)} %copy-done.2, f32[3,1024]{1,0:T(4,128)S(1)} %log_add_fusion), kind=kOutput, calls=%fused_computation.47 | convolution fusion | flops 409141248 | bytes 13381632 | tf_op jit(solution)/shard_map/while/body/eval_jaxpr/hst,she->the/dot_general | solution.py:165
  276.7 2.6 fusion.26
  279.3 3.7 fusion.7
  283.1 3.0 copy.42
  286.1 0.3 reduce-scatter.26.cloned.1.call-start
  286.4 4.3 fusion.13
  290.7 1.3 copy-done.19
  292.0 4.3 fusion.17
  296.4 1.3 copy-done.40
  297.8 4.3 fusion.19
  302.1 0.6 copy-done.34
  302.8 39.8 %all-reduce = (f32[768]{0:T(1024)}, f32[768]{0:T(1024)}, f32[768]{0:T(1024)}, f32[768]{0:T(1024)}) all-reduce(f32[768]{0:T(1024)S(1)} %copy-done.36, f32[768]{0:T(1024)S(1)} %copy-done.37, f32[768]{0:T(1024)S(1)} %copy-done.34, f32[768]{0:T(1024)S(1)} %copy-done.35), channel_id=1, replica_groups=mesh['dp'=8,'tp'=4] {'dp','tp'}, use_global_device_ids=true, to_apply=%region_21.22 | all-reduce | flops 3072 | bytes 24576 | tf_op jit(solution)/shard_map/psum | solution.py:197
  342.6 1.6 copy.41
  344.2 18.5 %reduce-scatter.20.cloned.1.call-done = bf16[1,256,768]{2,1,0:T(8,128)(2,1)} async-done(((bf16[1,1024,768]{2,1,0:T(8,128)(2,1)}), bf16[1,256,768]{2,1,0:T(8,128)(2,1)}) %reduce-scatter.20.cloned.1.call-update) | async-done | bytes 393232 | tf_op jit(solution)/shard_map/reduce_scatter | solution.py:187
  362.7 1.9 convert_add_fusion
  364.6 68.7 %reduce-scatter.28.cloned.1.call-done = f32[96,576]{1,0:T(8,128)} async-done(((f32[768,576]{1,0:T(8,128)}), f32[96,576]{1,0:T(8,128)}) %reduce-scatter.28.cloned.1.call-update) | async-done | bytes 221200
  433.3 1.1 copy.43
  434.4 0.9 copy.32
  435.3 70.7 %reduce-scatter.26.cloned.1.call-done = f32[768,96]{0,1:T(8,128)} async-done(((f32[768,768]{0,1:T(8,128)}), f32[768,96]{0,1:T(8,128)}) %reduce-scatter.26.cloned.1.call-update) | async-done | bytes 294928 | tf_op jit(solution)/shard_map/reduce_scatter | solution.py:195
  506.0 72.6 %reduce-scatter.24.cloned.1.call-done = f32[96,768]{1,0:T(8,128)} async-done(((f32[768,768]{1,0:T(8,128)}), f32[96,768]{1,0:T(8,128)}) %reduce-scatter.24.cloned.1.call-update) | async-done | bytes 294928 | tf_op jit(solution)/shard_map/reduce_scatter | solution.py:194
  578.7 72.8 %reduce-scatter.22.cloned.1.call-done = f32[96,768]{1,0:T(8,128)} async-done(((f32[768,768]{1,0:T(8,128)}), f32[96,768]{1,0:T(8,128)}) %reduce-scatter.22.cloned.1.call-update) | async-done | bytes 294928 | tf_op jit(solution)/shard_map/reduce_scatter | solution.py:193
  (131 shorter events, 1.8 us)
Async XLA Ops:
  7.2 110.6 %copy-start = (bf16[768,768]{1,0:T(8,128)(2,1)S(1)}, bf16[768,768]{1,0:T(8,128)(2,1)}, u32[]{:S(2)}) copy-start(bf16[768,768]{1,0:T(8,128)(2,1)} %param.18) | copy-start | bytes 3538948
  7.2 24.8 %all-gather.5.cloned.1.call-start = ((), (), s32[]{:S(2)}) async-start(), calls=%async_computation.9 | async-start | bytes 1966080 | tf_op jit(solution)/shard_map/all_gather | solution.py:74
  7.9 77.6 %reduce-scatter.14.cloned.1.call-start = ((), (), s32[]{:S(2)}) async-start(), calls=%async_computation.10 | async-start | bytes 3932160 | tf_op jit(solution)/shard_map/reduce_scatter | solution.py:100
  9.8 25.0 %copy-start.21 = (f32[1024,32]{0,1:T(8,128)}, f32[1024,32]{0,1:T(8,128)S(1)}, u32[]{:S(2)}) copy-start(f32[1024,32]{0,1:T(8,128)S(1)} %get-tuple-element.122) | copy-start | bytes 393220
  34.7 4.6 copy-start.5
  35.1 2.4 copy-start.6
  35.1 2.4 copy-start.8
  35.1 2.4 copy-start.10
  35.1 2.4 copy-start.12
  37.5 4.6 copy-start.2
  42.1 2.3 copy-start.28
  42.1 3.1 copy-start.24
  44.4 0.8 copy-start.16
  47.5 38.1 %copy-start.14 = (bf16[1,256,768]{2,1,0:T(8,128)(2,1)S(1)}, bf16[1,256,768]{2,1,0:T(8,128)(2,1)}, u32[]{:S(2)}) copy-start(bf16[1,256,768]{2,1,0:T(8,128)(2,1)} %param.12) | copy-start | bytes 1179652
  47.5 39.6 %copy-start.26 = (f32[768]{0:T(1024)S(1)}, f32[768]{0:T(1024)}, u32[]{:S(2)}) copy-start(f32[768]{0:T(1024)} %param.19) | copy-start | bytes 9220
  47.5 39.6 %copy-start.33 = (f32[768]{0:T(1024)S(1)}, f32[768]{0:T(1024)}, u32[]{:S(2)}) copy-start(f32[768]{0:T(1024)} %param.20) | copy-start | bytes 9220
  47.5 60.4 %all-gather.7.cloned.1.call-start = ((), (), s32[]{:S(2)}) async-start(), calls=%async_computation.11 | async-start | bytes 1966080 | tf_op jit(solution)/shard_map/all_gather | solution.py:106
  86.8 134.0 %copy-start.31 = (f32[256]{0:T(256)}, f32[256]{0:T(256)S(1)}, u32[]{:S(2)}) copy-start(f32[256]{0:T(256)S(1)} %broadcast_multiply_fusion.6) | copy-start | bytes 3076
  87.1 133.7 %copy-start.32 = (f32[256]{0:T(256)}, f32[256]{0:T(256)S(1)}, u32[]{:S(2)}) copy-start(f32[256]{0:T(256)S(1)} %add_rsqrt_fusion.1) | copy-start | bytes 3076
  88.1 60.5 %reduce-scatter.16.cloned.1.call-start = ((), (), s32[]{:S(2)}) async-start(), calls=%async_computation.12 | async-start | bytes 1966080 | tf_op jit(solution)/shard_map/reduce_scatter | solution.py:112
  107.9 3.3 copy-start.39
  111.1 5.4 copy-start.44
  116.6 1.2 copy-start.45
  120.4 29.8 %copy-start.4 = (bf16[1,256,768]{2,1,0:T(8,128)(2,1)S(1)}, bf16[1,256,768]{2,1,0:T(8,128)(2,1)}, u32[]{:S(2)}) copy-start(bf16[1,256,768]{2,1,0:T(8,128)(2,1)} %param.23) | copy-start | bytes 1179652
  120.4 29.8 %copy-start.30 = (f32[768]{0:T(1024)S(1)}, f32[768]{0:T(1024)}, u32[]{:S(2)}) copy-start(f32[768]{0:T(1024)} %param.21) | copy-start | bytes 9220
  120.4 51.6 %all-gather.9.cloned.1.call-start = ((), (), s32[]{:S(2)}) async-start(), calls=%async_computation.13 | async-start | bytes 1966080 | tf_op jit(solution)/shard_map/all_gather | solution.py:122
  152.2 68.6 %reduce-scatter.18.cloned.1.call-start = ((), (), s32[]{:S(2)}) async-start(), calls=%async_computation.14 | async-start | bytes 3932160 | tf_op jit(solution)/shard_map/reduce_scatter | solution.py:134
  172.0 5.5 copy-start.42
  177.4 1.5 copy-start.46
  177.5 1.7 copy-start.18
  177.5 2.2 copy-start.20
  182.8 38.1 %copy-start.38 = (f32[768]{0:T(1024)S(1)}, f32[768]{0:T(1024)}, u32[]{:S(2)}) copy-start(f32[768]{0:T(1024)} %param.22) | copy-start | bytes 9220
  182.8 41.2 %copy-start.27 = (f32[768]{0:T(1024)S(1)}, f32[768]{0:T(1024)}, u32[]{:S(2)}) copy-start(f32[768]{0:T(1024)} %param.19) | copy-start | bytes 9220
  182.8 62.8 %all-gather.11.cloned.1.call-start = ((), (), s32[]{:S(2)}) async-start(), calls=%async_computation.15 | async-start | bytes 1966080 | tf_op jit(solution)/shard_map/all_gather | solution.py:139
  224.0 1.8 copy-start.29
  224.0 21.6 %copy-start.25 = (bf16[192,768]{1,0:T(8,128)(2,1)S(1)}, bf16[192,768]{1,0:T(8,128)(2,1)}, u32[]{:S(2)}) copy-start(bf16[192,768]{1,0:T(8,128)(2,1)} %param.15) | copy-start | bytes 884740
  225.8 116.8 %reduce-scatter.30.cloned.1.call-start = ((), (), s32[]{:S(2)}) async-start(), calls=%async_computation.21 | async-start | bytes 884736
  247.7 6.3 slice-start
  247.7 7.3 %slice-start.1 = ((s8[12582912]{0:T(1024)(128)(4,1)}), s8[4194304]{0:T(1024)(128)(4,1)S(1)}, s32[]{:S(2)}) async-start(s8[12582912]{0:T(1024)(128)(4,1)} %bitcast.122), calls=%async_computation.23 | async-start | bytes 8388608
  247.7 8.5 %slice-start.2 = ((s8[12582912]{0:T(1024)(128)(4,1)}), s8[4194304]{0:T(1024)(128)(4,1)S(1)}, s32[]{:S(2)}) async-start(s8[12582912]{0:T(1024)(128)(4,1)} %bitcast.122), calls=%async_computation.24 | async-start | bytes 8388608
  256.2 5.3 copy-start.11
  256.2 5.3 copy-start.13
  261.4 5.0 copy-start.3
  261.4 5.0 copy-start.7
  261.5 5.0 copy-start.9
  266.5 1.4 copy-start.15
  266.5 1.5 copy-start.17
  267.9 1.7 copy-start.22
  267.9 1.7 copy-start.23
  269.6 93.1 %reduce-scatter.20.cloned.1.call-start = ((), (), s32[]{:S(2)}) async-start(), calls=%async_computation.16 | async-start | bytes 1966080 | tf_op jit(solution)/shard_map/reduce_scatter | solution.py:187
  270.0 6.7 %copy-start.43 = (bf16[768,3,192]{0,2,1:T(8,128)(2,1)S(1)}, bf16[768,3,192]{0,2,1:T(8,128)(2,1)}, u32[]{:S(2)}) copy-start(bf16[768,3,192]{0,2,1:T(8,128)(2,1)} %param.14) | copy-start | bytes 2654212
  279.3 154.0 %reduce-scatter.28.cloned.1.call-start = ((), (), s32[]{:S(2)}) async-start(), calls=%async_computation.20 | async-start | bytes 2211840
  283.1 3.3 copy-start.41
  286.1 219.9 %reduce-scatter.26.cloned.1.call-start = ((), (), s32[]{:S(2)}) async-start(), calls=%async_computation.19 | async-start | bytes 2654208 | tf_op jit(solution)/shard_map/reduce_scatter | solution.py:195
  290.6 1.4 copy-start.19
  290.7 288.0 %reduce-scatter.24.cloned.1.call-start = ((), (), s32[]{:S(2)}) async-start(), calls=%async_computation.18 | async-start | bytes 2654208 | tf_op jit(solution)/shard_map/reduce_scatter | solution.py:194
  296.3 1.4 copy-start.40
  296.4 355.1 %reduce-scatter.22.cloned.1.call-start = ((), (), s32[]{:S(2)}) async-start(), calls=%async_computation.17 | async-start | bytes 2654208 | tf_op jit(solution)/shard_map/reduce_scatter | solution.py:193
  302.1 0.7 copy-start.34
  302.1 0.7 copy-start.35
  302.1 0.7 copy-start.36
  302.1 0.7 copy-start.37
  302.1 349.4 %copy-start.1 = (bf16[768,768]{1,0:T(8,128)(2,1)S(1)}, bf16[768,768]{1,0:T(8,128)(2,1)}, u32[]{:S(2)}) copy-start(bf16[768,768]{1,0:T(8,128)(2,1)} %param.18) | copy-start | bytes 3538948
Sparse Core Ops, SparseCore 0:
  9.6 22.3 all-gather.4
  47.6 37.8 reduce-scatter.13
  88.2 19.6 all-gather.6
  120.5 27.9 reduce-scatter.15
  152.3 19.6 all-gather.8
  182.9 37.8 reduce-scatter.17
  225.9 19.6 all-gather.10
  269.7 63.2 reduce-scatter.29
  335.5 27.1 reduce-scatter.19
  366.0 67.2 reduce-scatter.27
  437.4 68.5 reduce-scatter.25
  509.9 68.6 reduce-scatter.23
  582.7 68.7 reduce-scatter.21
where the time goes:
time: 659 us; the launch traced here: 658 us
  waiting for transfers between devices  489 us (74%)
  matrix products  72.9 us (11%)
  blocking collectives  39.8 us (6%)
  other arithmetic  21.7 us (3%)
  local copies, waits for them, and re-layouts  18.2 us (3%)
  between operations  15.1 us (2%)
    reduce_scatter x1, waiting for transfers between devices, body(): lax.psum_scatter(gate_grad, 'dp', scatter_dimension=0, tiled=True)  72.8 us
    reduce_scatter x1, waiting for transfers between devices, body(): lax.psum_scatter(up_grad, 'dp', scatter_dimension=0, tiled=True)  72.6 us
    reduce_scatter x1, waiting for transfers between devices, body(): lax.psum_scatter(down_grad, 'dp', scatter_dimension=1, tiled=True)  70.7 us
    unnamed x15, waiting for transfers between devices  69.5 us
    psum x1, blocking collectives, body(): lax.psum((gain_one_part, bias_one_part, gain_two_part, bias_two_part), ('...  39.8 us
    reduce_scatter x1, waiting for transfers between devices, body(): lax.psum_scatter(attn_partial, 'tp', scatter_dimension=1, tiled=True)  38 us
    reduce_scatter x1, waiting for transfers between devices, body(): lax.psum_scatter(grad_inner, 'tp', scatter_dimension=1, tiled=True)  38 us
    reduce_scatter x1, waiting for transfers between devices, body(): lax.psum_scatter(ffn_partial.astype(jnp.bfloat16), 'tp', scatter_dimensio...  27.9 us
  transfers between devices with their start and end apart: 13, of which 12 were waited for; matrix products, arithmetic and copies ran while one was open for 5% of the time, Pallas kernels for 0%

commit v1 on v0

--- a/solution.py
+++ b/solution.py
@@ -71,7 +71,16 @@
     own_positions = offset + jnp.arange(piece_len, dtype=jnp.int32)
     row_valid = (own_positions[None, :] < lengths[:, None]).astype(jnp.float32)
     cosine, sine_table = angle_tables(seq_len, HD)
-    gathered = lax.all_gather(layer_input, "tp", axis=1, tiled=True)
+    ways = lax.axis_size("tp")
+    up = [(d, (d + 1) % ways) for d in range(ways)]
+    down = [(d, (d - 1) % ways) for d in range(ways)]
+    earlier, later = ([layer_input], [layer_input])
+    for _ in range(ways // 2):
+        earlier.append(lax.ppermute(earlier[-1], "tp", up))
+    for _ in range((ways - 1) // 2):
+        later.append(lax.ppermute(later[-1], "tp", down))
+    line = jnp.concatenate([*earlier[::-1], *later[1:]], axis=1)
+    gathered = jnp.roll(line, (lax.axis_index("tp") - ways // 2) * layer_input.shape[1], axis=1)
     projected = jnp.einsum("rsd,dce->rsce", gathered, w_qkv, preferred_element_type=jnp.float32)
     shaped = projected.reshape(row_count, seq_len, 3, heads_local, HD)
     queries = rotate(shaped[:, :, 0], cosine, sine_table, 1.0).astype(jnp.bfloat16)

time: 659 us -> 660 us (level)
    reduce_scatter x0 -> x1, waiting for transfers between devices: none -> 72.7 us  [body(): lax.psum_scatter(qkv_grad, 'dp', scatter_dimension=0, tiled=True)]
    unnamed x15 -> x13, waiting for transfers between devices: 69.5 us -> 0.2 us
    all_gather x1 -> x0, waiting for transfers between devices: 22.1 us -> none  [body(): gathered = lax.all_gather(layer_input, 'tp', axis=1, tiled=True)]
    ppermute x0 -> x3, waiting for transfers between devices: none -> 9.99 us  [the longest x2 9.99 us: body(): earlier.append(lax.ppermute(earlier[-1], 'tp', up))]
    unnamed x104 -> x120, local copies, waits for them, and re-layouts: 18.1 us -> 12.6 us
  transfers between devices with their start and end apart: 13 -> 15, of which waited for: 12 -> 13; matrix products, arithmetic and copies ran while one was open for 5% -> 5% of each run, Pallas kernels for 0% -> 0%
where the time goes in v1:
time: 660 us; the launch traced here: 659 us
  waiting for transfers between devices  490 us (74%)
  matrix products  73.3 us (11%)
  blocking collectives  39.8 us (6%)
  other arithmetic  21.7 us (3%)
  between operations  15.7 us (2%)
  local copies, waits for them, and re-layouts  12.8 us (2%)
    reduce_scatter x1, waiting for transfers between devices, body(): lax.psum_scatter(gate_grad, 'dp', scatter_dimension=0, tiled=True)  72.8 us
    reduce_scatter x1, waiting for transfers between devices, body(): lax.psum_scatter(qkv_grad, 'dp', scatter_dimension=0, tiled=True)  72.7 us
    reduce_scatter x1, waiting for transfers between devices, body(): lax.psum_scatter(up_grad, 'dp', scatter_dimension=0, tiled=True)  72.7 us
    reduce_scatter x1, waiting for transfers between devices, body(): lax.psum_scatter(down_grad, 'dp', scatter_dimension=1, tiled=True)  72 us
    reduce_scatter x1, waiting for transfers between devices, body(): lax.psum_scatter(attn_partial, 'tp', scatter_dimension=1, tiled=True)  41.8 us
    psum x1, blocking collectives, body(): lax.psum((gain_one_part, bias_one_part, gain_two_part, bias_two_part), ('...  39.8 us
    reduce_scatter x1, waiting for transfers between devices, body(): lax.psum_scatter(grad_inner, 'tp', scatter_dimension=1, tiled=True)  38 us
    reduce_scatter x1, waiting for transfers between devices, body(): lax.psum_scatter(ffn_partial.astype(jnp.bfloat16), 'tp', scatter_dimensio...  28.1 us
  transfers between devices with their start and end apart: 15, of which 13 were waited for; matrix products, arithmetic and copies ran while one was open for 5% of the time, Pallas kernels for 0%

profile of v1, /device:TPU:0, one launch (start us, length us, event | category | flops | bytes accessed | tf_op | source)
XLA Modules:
  0.0 659.0 jit_solution(965289056649639988)
XLA Ops:
  7.3 0.5 collective-permute-start
  7.8 2.0 collective-permute-start.2
  9.8 7.2 %collective-permute-done = bf16[1,256,768]{2,1,0:T(8,128)(2,1)S(1)} collective-permute-done((bf16[1,256,768]{2,1,0:T(8,128)(2,1)}, bf16[1,256,768]{2,1,0:T(8,128)(2,1)S(1)}, u32[]{:S(2)}, u32[]{:S(2)}) %collective-permute-start) | collective-permute-done | bytes 393248 | tf_op jit(solution)/shard_map/ppermute | solution.py:79
  17.0 2.6 collective-permute-start.1
  20.2 1.2 broadcast_multiply_fusion
  21.5 2.8 collective-permute-done.1
  24.3 1.0 constant_dynamic-update-slice_fusion.5
  25.5 1.7 copy-done.36
  27.2 1.1 convolution_bitcast_fusion.1
  28.5 0.2 fusion.46
  28.8 2.4 fusion.68
  31.2 1.7 fusion
  33.0 2.8 copy-done.2
  35.8 2.3 fusion.40
  38.1 0.8 copy-done.16
  38.9 2.3 convolution_bitcast_fusion
  41.2 41.8 %reduce-scatter.12.cloned.1.call-done = f32[1,256,768]{2,1,0:T(8,128)} async-done(((f32[1,1024,768]{2,1,0:T(8,128)}), f32[1,256,768]{2,1,0:T(8,128)}) %reduce-scatter.12.cloned.1.call-update) | async-done | bytes 786448 | tf_op jit(solution)/shard_map/reduce_scatter | solution.py:109
  83.0 1.3 fusion.67
  84.6 0.9 fusion.44
  85.6 0.2 reduce-scatter.14.cloned.1.call-start
  85.8 19.5 %all-gather.4.cloned.1.call-done = bf16[1,1024,768]{2,1,0:T(8,128)(2,1)} async-done(((bf16[1,256,768]{2,1,0:T(8,128)(2,1)}), bf16[1,1024,768]{2,1,0:T(8,128)(2,1)}) %all-gather.4.cloned.1.call-update) | async-done | bytes 1572880 | tf_op jit(solution)/shard_map/all_gather | solution.py:115
  105.4 3.3 fusion.23
  108.6 5.4 multiply_convert_fusion.3
  114.1 1.1 copy-done.51
  115.2 2.6 fusion.25
  117.9 28.1 %reduce-scatter.14.cloned.1.call-done = bf16[1,256,768]{2,1,0:T(8,128)(2,1)} async-done(((bf16[1,1024,768]{2,1,0:T(8,128)(2,1)}), bf16[1,256,768]{2,1,0:T(8,128)(2,1)}) %reduce-scatter.14.cloned.1.call-update) | async-done | bytes 393232 | tf_op jit(solution)/shard_map/reduce_scatter | solution.py:121
  146.0 1.3 fusion.66
  147.3 0.2 multiply_reduce_fusion.5
  147.6 1.0 multiply_reduce_fusion.1
  148.5 1.1 fusion.63
  149.7 19.7 %all-gather.6.cloned.1.call-done = bf16[1,1024,768]{2,1,0:T(8,128)(2,1)} async-done(((bf16[1,256,768]{2,1,0:T(8,128)(2,1)}), bf16[1,1024,768]{2,1,0:T(8,128)(2,1)}) %all-gather.6.cloned.1.call-update) | async-done | bytes 1572880 | tf_op jit(solution)/shard_map/all_gather | solution.py:131
  169.4 5.4 multiply_convert_fusion.1
  174.9 1.4 fusion.69
  176.5 0.5 copy-done.20
  177.0 3.1 add_bitcast_fusion
  180.3 38.0 %reduce-scatter.16.cloned.1.call-done = f32[1,256,768]{2,1,0:T(8,128)} async-done(((f32[1,1024,768]{2,1,0:T(8,128)}), f32[1,256,768]{2,1,0:T(8,128)}) %reduce-scatter.16.cloned.1.call-update) | async-done | bytes 786448 | tf_op jit(solution)/shard_map/reduce_scatter | solution.py:143
  218.2 3.2 multiply_reduce_fusion.2
  221.4 1.7 fusion.64
  223.2 0.3 reduce-scatter.28.cloned.1.call-start
  223.5 19.5 %all-gather.8.cloned.1.call-done = bf16[1,1024,768]{2,1,0:T(8,128)(2,1)} async-done(((bf16[1,256,768]{2,1,0:T(8,128)(2,1)}), bf16[1,1024,768]{2,1,0:T(8,128)(2,1)}) %all-gather.8.cloned.1.call-update) | async-done | bytes 1572880 | tf_op jit(solution)/shard_map/all_gather | solution.py:148
  242.9 2.1 fusion.34
  245.0 6.3 multiply_reduce_fusion
  251.3 1.0 slice-done.1
  252.3 1.2 slice-done.2
  253.5 5.3 multiply_convert_fusion
  258.8 5.0 fusion.29
  263.8 1.2 fusion.30
  265.3 1.6 fusion.31
  267.0 0.2 subtract_convert_fusion.1
  267.3 6.9 %fusion.37 = bf16[3,64,1024]{2,1,0:T(8,128)(2,1)S(1)} fusion(bf16[1024,3,64]{0,2,1:T(8,128)(2,1)S(1)} %bitcast.121, f32[3,1024,1024]{1,2,0:T(8,128)} %copy-done.2, f32[3,1024]{1,0:T(4,128)S(1)} %log_add_fusion), kind=kOutput, calls=%fused_computation.49 | convolution fusion | flops 409141248 | bytes 13381632 | tf_op jit(solution)/shard_map/while/body/eval_jaxpr/hst,she->the/dot_general | solution.py:174
  274.2 2.6 fusion.26
  276.9 4.9 fusion.13
  281.8 0.3 reduce-scatter.24.cloned.1.call-start
  282.1 4.3 fusion.17
  286.6 4.9 fusion.19
  291.6 4.4 fusion.6
  296.1 39.8 %all-reduce = (f32[768]{0:T(1024)}, f32[768]{0:T(1024)}, f32[768]{0:T(1024)}, f32[768]{0:T(1024)}) all-reduce(f32[768]{0:T(1024)S(1)} %copy-done.43, f32[768]{0:T(1024)S(1)} %copy-done.44, f32[768]{0:T(1024)S(1)} %copy-done.41, f32[768]{0:T(1024)S(1)} %copy-done.42), channel_id=1, replica_groups=mesh['dp'=8,'tp'=4] {'dp','tp'}, use_global_device_ids=true, to_apply=%region_21.22 | all-reduce | flops 3072 | bytes 24576 | tf_op jit(solution)/shard_map/psum | solution.py:206
  335.9 1.6 copy.41
  337.5 22.5 %reduce-scatter.18.cloned.1.call-done = bf16[1,256,768]{2,1,0:T(8,128)(2,1)} async-done(((bf16[1,1024,768]{2,1,0:T(8,128)(2,1)}), bf16[1,256,768]{2,1,0:T(8,128)(2,1)}) %reduce-scatter.18.cloned.1.call-update) | async-done | bytes 393232 | tf_op jit(solution)/shard_map/reduce_scatter | solution.py:196
  360.0 1.9 convert_add_fusion
  361.9 72.0 %reduce-scatter.26.cloned.1.call-done = f32[768,96]{0,1:T(8,128)} async-done(((f32[768,768]{0,1:T(8,128)}), f32[768,96]{0,1:T(8,128)}) %reduce-scatter.26.cloned.1.call-update) | async-done | bytes 294928 | tf_op jit(solution)/shard_map/reduce_scatter | solution.py:204
  433.9 72.7 %reduce-scatter.24.cloned.1.call-done = f32[96,768]{1,0:T(8,128)} async-done(((f32[768,768]{1,0:T(8,128)}), f32[96,768]{1,0:T(8,128)}) %reduce-scatter.24.cloned.1.call-update) | async-done | bytes 294928 | tf_op jit(solution)/shard_map/reduce_scatter | solution.py:203
  506.6 72.8 %reduce-scatter.22.cloned.1.call-done = f32[96,768]{1,0:T(8,128)} async-done(((f32[768,768]{1,0:T(8,128)}), f32[96,768]{1,0:T(8,128)}) %reduce-scatter.22.cloned.1.call-update) | async-done | bytes 294928 | tf_op jit(solution)/shard_map/reduce_scatter | solution.py:202
  579.4 72.7 %reduce-scatter.20.cloned.1.call-done = f32[96,3,192]{2,0,1:T(8,128)} async-done(((f32[768,3,192]{2,0,1:T(8,128)}), f32[96,3,192]{2,0,1:T(8,128)}) %reduce-scatter.20.cloned.1.call-update) | async-done | bytes 221200 | tf_op jit(solution)/shard_map/reduce_scatter | solution.py:200
  (151 shorter events, 1.9 us)
Async XLA Ops:
  7.2 108.0 %copy-start = (bf16[768,768]{1,0:T(8,128)(2,1)S(1)}, bf16[768,768]{1,0:T(8,128)(2,1)}, u32[]{:S(2)}) copy-start(bf16[768,768]{1,0:T(8,128)(2,1)} %param.18) | copy-start | bytes 3538948
  7.2 18.3 %copy-start.4 = (bf16[1,256,768]{2,1,0:T(8,128)(2,1)S(1)}, bf16[1,256,768]{2,1,0:T(8,128)(2,1)}, u32[]{:S(2)}) copy-start(bf16[1,256,768]{2,1,0:T(8,128)(2,1)} %param.12) | copy-start | bytes 1179652
  7.2 75.8 %reduce-scatter.12.cloned.1.call-start = ((), (), s32[]{:S(2)}) async-start(), calls=%async_computation.9 | async-start | bytes 3932160 | tf_op jit(solution)/shard_map/reduce_scatter | solution.py:109
  7.3 9.8 %collective-permute-start = (bf16[1,256,768]{2,1,0:T(8,128)(2,1)}, bf16[1,256,768]{2,1,0:T(8,128)(2,1)S(1)}, u32[]{:S(2)}, u32[]{:S(2)}) collective-permute-start(bf16[1,256,768]{2,1,0:T(8,128)(2,1)} %param.12), channel_id=1, source_target_pairs={{0,1},{1,2},{2,3},{3,0},{4,5},{5,6},{6,7},{7,4},{8,9},{9,10},{10,1... | collective-permute-start | bytes 1179656 | tf_op jit(solution)/shard_map/ppermute | solution.py:79
  7.8 17.5 %collective-permute-start.2 = (bf16[1,256,768]{2,1,0:T(8,128)(2,1)}, bf16[1,256,768]{2,1,0:T(8,128)(2,1)S(1)}, u32[]{:S(2)}, u32[]{:S(2)}) collective-permute-start(bf16[1,256,768]{2,1,0:T(8,128)(2,1)} %param.12), channel_id=1, source_target_pairs={{0,3},{1,0},{2,1},{3,2},{4,7},{5,4},{6,5},{7,6},{8,11},{9,8},{10,9... | collective-permute-start | bytes 1179656 | tf_op jit(solution)/shard_map/ppermute | solution.py:81
  17.0 7.2 %collective-permute-start.1 = (bf16[1,256,768]{2,1,0:T(8,128)(2,1)S(1)}, bf16[1,256,768]{2,1,0:T(8,128)(2,1)S(1)}, u32[]{:S(2)}, u32[]{:S(2)}) collective-permute-start(bf16[1,256,768]{2,1,0:T(8,128)(2,1)S(1)} %collective-permute-done), channel_id=1, source_target_pairs={{0,1},{1,2},{2,3},{3,0},{4,5},{5,6},{6,7},{7,4},{8,9},{9,10},{10,1... | collective-permute-start | bytes 1179656 | tf_op jit(solution)/shard_map/ppermute | solution.py:79
  21.5 7.1 %copy-start.21 = (f32[1024,32]{0,1:T(8,128)}, f32[1024,32]{0,1:T(8,128)S(1)}, u32[]{:S(2)}) copy-start(f32[1024,32]{0,1:T(8,128)S(1)} %get-tuple-element.100) | copy-start | bytes 393220
  21.5 5.8 copy-start.48
  28.3 4.7 copy-start.6
  28.8 2.4 copy-start.7
  28.8 2.4 copy-start.9
  28.8 2.4 copy-start.11
  28.8 2.4 copy-start.13
  31.2 4.5 copy-start.2
  35.8 2.3 copy-start.34
  35.8 3.1 copy-start.30
  41.1 43.4 %copy-start.32 = (f32[768]{0:T(1024)S(1)}, f32[768]{0:T(1024)}, u32[]{:S(2)}) copy-start(f32[768]{0:T(1024)} %param.19) | copy-start | bytes 9220
  41.1 43.5 %copy-start.40 = (f32[768]{0:T(1024)S(1)}, f32[768]{0:T(1024)}, u32[]{:S(2)}) copy-start(f32[768]{0:T(1024)} %param.20) | copy-start | bytes 9220
  41.2 64.2 %all-gather.4.cloned.1.call-start = ((), (), s32[]{:S(2)}) async-start(), calls=%async_computation.10 | async-start | bytes 1966080 | tf_op jit(solution)/shard_map/all_gather | solution.py:115
  84.3 133.9 %copy-start.38 = (f32[256]{0:T(256)}, f32[256]{0:T(256)S(1)}, u32[]{:S(2)}) copy-start(f32[256]{0:T(256)S(1)} %broadcast_multiply_fusion.6) | copy-start | bytes 3076
  84.6 133.6 %copy-start.39 = (f32[256]{0:T(256)}, f32[256]{0:T(256)S(1)}, u32[]{:S(2)}) copy-start(f32[256]{0:T(256)S(1)} %add_rsqrt_fusion.1) | copy-start | bytes 3076
  85.6 60.4 %reduce-scatter.14.cloned.1.call-start = ((), (), s32[]{:S(2)}) async-start(), calls=%async_computation.11 | async-start | bytes 1966080 | tf_op jit(solution)/shard_map/reduce_scatter | solution.py:121
  105.4 3.3 copy-start.46
  108.6 5.4 copy-start.50
  117.8 29.8 %copy-start.5 = (bf16[1,256,768]{2,1,0:T(8,128)(2,1)S(1)}, bf16[1,256,768]{2,1,0:T(8,128)(2,1)}, u32[]{:S(2)}) copy-start(bf16[1,256,768]{2,1,0:T(8,128)(2,1)} %param.23) | copy-start | bytes 1179652
  117.8 29.8 %copy-start.37 = (f32[768]{0:T(1024)S(1)}, f32[768]{0:T(1024)}, u32[]{:S(2)}) copy-start(f32[768]{0:T(1024)} %param.21) | copy-start | bytes 9220
  117.8 51.6 %all-gather.6.cloned.1.call-start = ((), (), s32[]{:S(2)}) async-start(), calls=%async_computation.12 | async-start | bytes 1966080 | tf_op jit(solution)/shard_map/all_gather | solution.py:131
  149.6 68.6 %reduce-scatter.16.cloned.1.call-start = ((), (), s32[]{:S(2)}) async-start(), calls=%async_computation.13 | async-start | bytes 3932160 | tf_op jit(solution)/shard_map/reduce_scatter | solution.py:143
  169.4 5.5 copy-start.47
  174.9 2.2 copy-start.20
  180.2 38.1 %copy-start.45 = (f32[768]{0:T(1024)S(1)}, f32[768]{0:T(1024)}, u32[]{:S(2)}) copy-start(f32[768]{0:T(1024)} %param.22) | copy-start | bytes 9220
  180.2 41.3 %copy-start.33 = (f32[768]{0:T(1024)S(1)}, f32[768]{0:T(1024)}, u32[]{:S(2)}) copy-start(f32[768]{0:T(1024)} %param.19) | copy-start | bytes 9220
  180.2 43.2 %copy-start.35 = (f32[3,1024]{1,0:T(4,128)S(1)}, f32[3,1024]{1,0:T(4,128)}, u32[]{:S(2)}) copy-start(f32[3,1024]{1,0:T(4,128)} %copy-done.34) | copy-start | bytes 36868
  180.2 62.7 %copy-start.31 = (bf16[192,768]{1,0:T(8,128)(2,1)S(1)}, bf16[192,768]{1,0:T(8,128)(2,1)}, u32[]{:S(2)}) copy-start(bf16[192,768]{1,0:T(8,128)(2,1)} %param.15) | copy-start | bytes 884740
  180.2 62.7 %all-gather.8.cloned.1.call-start = ((), (), s32[]{:S(2)}) async-start(), calls=%async_computation.14 | async-start | bytes 1966080 | tf_op jit(solution)/shard_map/all_gather | solution.py:148
  223.2 112.7 %reduce-scatter.28.cloned.1.call-start = ((), (), s32[]{:S(2)}) async-start(), calls=%async_computation.20 | async-start | bytes 884736
  245.0 6.3 slice-start
  245.0 7.3 %slice-start.1 = ((s8[12582912]{0:T(1024)(128)(4,1)}), s8[4194304]{0:T(1024)(128)(4,1)S(1)}, s32[]{:S(2)}) async-start(s8[12582912]{0:T(1024)(128)(4,1)} %bitcast.118), calls=%async_computation.22 | async-start | bytes 8388608
  245.0 8.5 %slice-start.2 = ((s8[12582912]{0:T(1024)(128)(4,1)}), s8[4194304]{0:T(1024)(128)(4,1)S(1)}, s32[]{:S(2)}) async-start(s8[12582912]{0:T(1024)(128)(4,1)} %bitcast.118), calls=%async_computation.23 | async-start | bytes 8388608
  253.5 5.3 copy-start.12
  253.5 5.3 copy-start.14
  258.8 5.0 copy-start.3
  258.8 5.0 copy-start.8
  258.8 5.0 copy-start.10
  265.3 1.7 copy-start.22
  265.3 1.7 copy-start.23
  266.9 93.1 %reduce-scatter.18.cloned.1.call-start = ((), (), s32[]{:S(2)}) async-start(), calls=%async_computation.15 | async-start | bytes 1966080 | tf_op jit(solution)/shard_map/reduce_scatter | solution.py:196
  267.3 6.9 %copy-start.26 = (bf16[1,1024,3,64]{1,3,2,0:T(8,128)(2,1)}, bf16[1,1024,3,64]{1,3,2,0:T(8,128)(2,1)S(1)}, u32[]{:S(2)}) copy-start(bf16[1,1024,3,64]{1,3,2,0:T(8,128)(2,1)S(1)} %pad_maximum_fusion.5) | copy-start | bytes 1179652
  267.3 6.9 %copy-start.28 = (bf16[1,1024,3,64]{1,3,2,0:T(8,128)(2,1)}, bf16[1,1024,3,64]{1,3,2,0:T(8,128)(2,1)S(1)}, u32[]{:S(2)}) copy-start(bf16[1,1024,3,64]{1,3,2,0:T(8,128)(2,1)S(1)} %pad_maximum_fusion.6) | copy-start | bytes 1179652
  267.3 6.9 %copy-start.49 = (bf16[768,3,192]{0,2,1:T(8,128)(2,1)S(1)}, bf16[768,3,192]{0,2,1:T(8,128)(2,1)}, u32[]{:S(2)}) copy-start(bf16[768,3,192]{0,2,1:T(8,128)(2,1)} %param.14) | copy-start | bytes 2654212
  274.2 2.7 copy-start.24
  276.9 5.2 copy-start.19
  276.9 157.0 %reduce-scatter.26.cloned.1.call-start = ((), (), s32[]{:S(2)}) async-start(), calls=%async_computation.19 | async-start | bytes 2654208 | tf_op jit(solution)/shard_map/reduce_scatter | solution.py:204
  281.8 224.8 %reduce-scatter.24.cloned.1.call-start = ((), (), s32[]{:S(2)}) async-start(), calls=%async_computation.18 | async-start | bytes 2654208 | tf_op jit(solution)/shard_map/reduce_scatter | solution.py:203
  286.5 5.1 copy-start.25
  286.5 5.1 copy-start.27
  286.5 5.1 copy-start.29
  286.5 292.9 %reduce-scatter.22.cloned.1.call-start = ((), (), s32[]{:S(2)}) async-start(), calls=%async_computation.17 | async-start | bytes 2654208 | tf_op jit(solution)/shard_map/reduce_scatter | solution.py:202
  291.5 4.6 copy-start.41
  291.5 4.6 copy-start.42
  291.5 4.6 copy-start.43
  291.5 4.6 copy-start.44
  291.5 360.6 %reduce-scatter.20.cloned.1.call-start = ((), (), s32[]{:S(2)}) async-start(), calls=%async_computation.16 | async-start | bytes 2654208 | tf_op jit(solution)/shard_map/reduce_scatter | solution.py:200
  291.6 360.5 %copy-start.1 = (bf16[768,768]{1,0:T(8,128)(2,1)S(1)}, bf16[768,768]{1,0:T(8,128)(2,1)}, u32[]{:S(2)}) copy-start(bf16[768,768]{1,0:T(8,128)(2,1)} %param.18) | copy-start | bytes 3538948
  (7 other events, 9.6 us)
Sparse Core Ops, SparseCore 0:
  41.3 41.7 reduce-scatter.11
  85.7 19.6 all-gather.3
  117.9 27.9 reduce-scatter.13
  149.8 19.6 all-gather.5
  180.3 37.8 reduce-scatter.15
  223.3 19.6 all-gather.7
  267.1 63.2 reduce-scatter.27
  332.9 27.0 reduce-scatter.17
  364.1 69.7 reduce-scatter.25
  437.8 68.7 reduce-scatter.23
  510.7 68.7 reduce-scatter.21
  583.3 68.7 reduce-scatter.19
